TPU v7x, 32 devices: a whole 2x2x4 slice. The times are simulated.
32 devices in a mesh: jpair: 2 (over x), blk: 16 (over z, y, core).
Axes of the slice: x: 2, y: 2, z: 4, core: 2. Of those that a mesh axis runs over, the one named last changes fastest.
Arguments:
- dipole: bfloat16 [256, 12, 3, 256, 256], P('blk'), may hold values from -24 to 24
- block_cols: int32 [256, 12], P('blk'), may hold values from 0 to 255, as said below
- upper_vecs: bfloat16 [131072, 256], P(('jpair', 'blk')), parts along dimension 0, may hold values from -0.0234375 to 0.0234375
- lower_vecs: bfloat16 [131072, 128], P(('jpair', 'blk')), parts along dimension 0, may hold values from -0.0234375 to 0.0234375
- upper_energy: float32 [512], P('jpair'), parts along dimension 0, may hold values from 1 to 2
- lower_energy: float32 [256], P('jpair'), parts along dimension 0, may hold values from 0 to 0.8
Outputs:
- strength: float32 [512, 128], P(('jpair', 'blk')), parts along dimension 0
- intensity: float32 [512, 128], P(('jpair', 'blk')), parts along dimension 0
There are 2 independent parts, one for each index of `jpair`. A program takes and returns all parts, laid end to end along the dimension named above; an argument that names none is the same for every part. Nothing has to cross between parts.
Inputs may be any that keep to these rules, and one draw needn't show every extreme that they name: `block_cols`: within one block row the 12 block columns are distinct, and one of them is the row's own index. Splitting the block rows into 16 equal runs of consecutive rows, the columns of one run that fall in another run number at most 12 distinct blocks for each other run, and exactly 12 for some.
All inputs are finite; a program needn't handle non-finite values.
Results may differ from a plain program's by a relative error of at most 0.0026.
Values may be sent and summed in bfloat16 or wider, within the bound.
A program may use at most 256 MiB of HBM per device.

v0:
```python
import jax
import jax.numpy as jnp
from jax import lax
from jax.sharding import PartitionSpec as P

THERMAL = 0.3


def per_device(dipole, block_cols, upper_vecs, lower_vecs, upper_energy, lower_energy):
    rows_blk, nonzero, n_comps, block_size, _ = dipole.shape
    upper_count = upper_vecs.shape[1]
    lower_count = lower_vecs.shape[1]
    upper_blocks = upper_vecs.reshape(rows_blk, block_size, upper_count)
    halves = jnp.einsum(
        "rkast,rsu->rkatu", dipole, upper_blocks, preferred_element_type=jnp.float32
    ).astype(jnp.bfloat16)
    entry_count = rows_blk * nonzero
    halves = halves.reshape(entry_count, n_comps, block_size, upper_count)
    columns = block_cols.reshape(entry_count)
    group_size = lax.axis_size("blk")
    my_index = lax.axis_index("blk")
    gathered = lax.all_gather(lower_vecs, "blk", axis=0, tiled=True)
    all_blocks = gathered.reshape(gathered.shape[0] // block_size, block_size, lower_count)
    lows = jnp.take(all_blocks, columns, axis=0)
    proj = jnp.einsum("eatu,etl->aul", halves, lows, preferred_element_type=jnp.float32)
    share_rows = upper_count // group_size
    first_row = my_index * share_rows
    summed = lax.psum(proj, "blk")
    own_share = lax.dynamic_slice_in_dim(summed, first_row, share_rows, 1)
    strength = jnp.sum(own_share * own_share, axis=0)
    energy_rows = lax.dynamic_slice_in_dim(upper_energy, first_row, share_rows, 0)
    wavenumber = energy_rows[:, None] - lower_energy[None, :]
    intensity = wavenumber**3 * jnp.exp(-lower_energy / THERMAL)[None, :] * strength
    return (strength, intensity)


def solution(mesh):
    placed = (
        P("blk", None, None, None, None),
        P("blk", None),
        P(("jpair", "blk"), None),
        P(("jpair", "blk"), None),
        P("jpair"),
        P("jpair"),
    )
    return jax.shard_map(
        per_device,
        mesh=mesh,
        in_specs=placed,
        out_specs=(P(("jpair", "blk"), None), P(("jpair", "blk"), None)),
        check_vma=False,
    )
```

profile of v0, /device:TPU:0, one launch (start us, length us, event | category | flops | bytes accessed | tf_op | source)
XLA Modules:
  0.0 283.5 jit_solution(16496702931421474902)
XLA Ops:
  7.2 0.0 copy-start
  7.2 0.0 all-gather.2.cloned.1.call-start
  7.2 0.7 all-gather.2.cloned.1.call-update
  7.9 0.0 all-reduce.2.cloned.1.call-start
  8.0 0.8 reshape.59
  8.8 0.8 reshape.57
  9.5 0.8 dynamic_slice.7
  10.3 0.0 copy-done
  10.3 59.0 %convolution_convert_fusion = bf16[16,12,3,256,256]{4,3,2,1,0:T(8,128)(2,1)} fusion(bf16[16,12,3,256,256]{4,3,2,1,0:T(8,128)(2,1)} %param.6, bf16[16,256,256,1,1]{2,1,4,3,0:T(8,128)(2,1)S(1)} %bitcast.20), kind=kOutput, calls=%fused_computation.1 | convolution fusion | flops 19365101568 | bytes 153092096 | tf_op jit(solution)/shard_map/rkast,rsu->rkatu/dot_general | solution.py:14
  69.4 70.4 %all-gather.2.cloned.1.call-done = bf16[65536,128]{1,0:T(8,128)(2,1)} async-done(((bf16[4096,128]{1,0:T(8,128)(2,1)}), bf16[65536,128]{1,0:T(8,128)(2,1)}) %all-gather.2.cloned.1.call-update) | async-done | bytes 16777232 | tf_op jit(solution)/shard_map/all_gather | solution.py:22
  139.8 13.9 %gather_fusion = bf16[192,256,128]{2,1,0:T(8,128)(2,1)} fusion(bf16[256,256,128]{2,1,0:T(8,128)(2,1)} %bitcast.21, s32[1024]{0:T(1024)S(1)} %pad_clamp_fusion), kind=kCustom, calls=%fused_computation | custom fusion | bytes 25166592 | tf_op jit(solution)/shard_map/jit(_take)/gather | solution.py:24
  153.7 0.0 copy-start.2
  153.8 32.8 %fusion.5 = f32[3,256,128]{2,1,0:T(8,128)} fusion(bf16[192,3,256,256]{3,2,1,0:T(8,128)(2,1)} %bitcast.3, bf16[192,256,128]{2,1,0:T(8,128)(2,1)} %gather_fusion, pred[192]{0:T(512)(128)(4,1)S(1)} %compare_and_fusion), kind=kOutput, calls=%fused_computation.7 | convolution fusion | flops 9669967872 | bytes 88473792 | tf_op jit(solution)/shard_map/eatu,etl->aul/dot_general | solution.py:25
  186.6 0.0 all-reduce.2.cloned.1.call-update
  186.6 0.0 copy-done.2
  186.6 88.6 %all-reduce.2.cloned.1.call-done = f32[3,256,128]{2,1,0:T(8,128)} async-done(((f32[3,256,128]{2,1,0:T(8,128)}), f32[3,256,128]{2,1,0:T(8,128)}) %all-reduce.2.cloned.1.call-update) | async-done | bytes 393232 | tf_op jit(solution)/shard_map/psum | solution.py:28
  275.2 0.7 multiply_reduce_fusion
  276.0 0.0 copy-start.1
  276.0 0.7 fusion.9
  276.7 0.0 copy-done.1
  (4 shorter events, 0.0 us)
Async XLA Ops:
  7.2 3.2 %copy-start = (bf16[4096,256]{1,0:T(8,128)(2,1)S(1)}, bf16[4096,256]{1,0:T(8,128)(2,1)}, u32[]{:S(2)}) copy-start(bf16[4096,256]{1,0:T(8,128)(2,1)} %param.8) | copy-start | bytes 6291460
  7.2 132.6 %all-gather.2.cloned.1.call-start = ((), (), s32[]{:S(2)}) async-start(), calls=%async_computation | async-start | bytes 17825792 | tf_op jit(solution)/shard_map/all_gather | solution.py:22
  7.9 267.3 %all-reduce.2.cloned.1.call-start = ((), (), s32[]{:S(2)}) async-start(), calls=%async_computation.1 | async-start | bytes 786432 | tf_op jit(solution)/shard_map/psum | solution.py:28
  153.7 32.8 %copy-start.2 = (f32[128]{0:T(128)S(1)}, f32[128]{0:T(128)}, u32[]{:S(2)}) copy-start(f32[128]{0:T(128)} %param.11) | copy-start | bytes 1540
  276.0 0.7 copy-start.1
Sparse Core Ops, SparseCore 0:
  10.2 129.5 all-gather.1
  186.7 88.4 all-reduce.1
where the time goes:
time: 284 us; the launch traced here: 283 us
  waiting for transfers between devices  160 us (56%)
  matrix products  91.9 us (32%)
  local copies, waits for them, and re-layouts  16.3 us (6%)
  between operations  14.1 us (5%)
    psum x1, waiting for transfers between devices, per_device(): summed = lax.psum(proj, 'blk')  88.6 us
    all_gather x1, waiting for transfers between devices, per_device(): gathered = lax.all_gather(lower_vecs, 'blk', axis=0, tiled=True)  70.4 us
    dot_general x1, matrix products, per_device(): jnp.einsum('rkast,rsu->rkatu', dipole, upper_blocks, preferred_element_ty...  59 us
    dot_general x1, matrix products, per_device(): jnp.einsum('eatu,etl->aul', halves, lows, preferred_element_type=jnp.floa...  32.8 us
    gather x1, local copies, waits for them, and re-layouts, per_device(): lows = jnp.take(all_blocks, columns, axis=0)  13.9 us
  transfers between devices with their start and end apart: 2, of which 2 were waited for; matrix products, arithmetic and copies ran while one was open for 22% of the time, Pallas kernels for 0%

commit v1 on v0

--- a/solution.py
+++ b/solution.py
@@ -4,6 +4,28 @@
 from jax.sharding import PartitionSpec as P
 
 THERMAL = 0.3
+
+
+def laid_out(pieces, dim):
+    lengths = list(pieces.shape[1:])
+    lengths[dim] *= pieces.shape[0]
+    return jnp.moveaxis(pieces, 0, dim).reshape(lengths)
+
+
+def collect(x, axis, dim):
+    size = lax.axis_size(axis)
+    pairs = [(i, (i + 1) % size) for i in range(size)]
+    back = [(b, a) for a, b in pairs]
+    lower, upper = ([], [])
+    for lap in range(size - 1):
+        if lap % 2 == 0:
+            lower.append(lax.ppermute(lower[-1] if lower else x, axis, pairs))
+        else:
+            upper.append(lax.ppermute(upper[-1] if upper else x, axis, back))
+    blocks = jnp.stack([*lower[::-1], x, *upper])
+    shift = lax.axis_index(axis) - len(lower)
+    blocks = blocks[(jnp.arange(size) - shift) % size]
+    return laid_out(blocks, dim)
 
 
 def per_device(dipole, block_cols, upper_vecs, lower_vecs, upper_energy, lower_energy):
@@ -19,7 +41,7 @@
     columns = block_cols.reshape(entry_count)
     group_size = lax.axis_size("blk")
     my_index = lax.axis_index("blk")
-    gathered = lax.all_gather(lower_vecs, "blk", axis=0, tiled=True)
+    gathered = collect(lower_vecs, "blk", 0)
     all_blocks = gathered.reshape(gathered.shape[0] // block_size, block_size, lower_count)
     lows = jnp.take(all_blocks, columns, axis=0)
     proj = jnp.einsum("eatu,etl->aul", halves, lows, preferred_element_type=jnp.float32)

time: 284 us -> 423 us (1.49)
  starting transfers between devices: 0.08 us -> 110 us
  local copies, waits for them, and re-layouts: 16.3 us -> 61.9 us
  waiting for transfers between devices: 160 us -> 144 us
    ppermute x0 -> x15, starting transfers between devices: none -> 110 us  [the longest x8 105 us: collect(): lower.append(lax.ppermute(lower[-1] if lower else x, axis, pairs))]
    all_gather x1 -> x0, waiting for transfers between devices: 70.4 us -> none  [per_device(): gathered = lax.all_gather(lower_vecs, 'blk', axis=0, tiled=True)]
    ppermute x0 -> x15, waiting for transfers between devices: none -> 50.8 us  [the longest x8 50.8 us: collect(): lower.append(lax.ppermute(lower[-1] if lower else x, axis, pairs))]
    unnamed x6 -> x55, local copies, waits for them, and re-layouts: 0.02 us -> 33.5 us
    gather x0 -> x1, local copies, waits for them, and re-layouts: none -> 13.1 us  [collect(): blocks = blocks[(jnp.arange(size) - shift) % size]]
    psum x1, waiting for transfers between devices: 88.6 us -> 93 us  [per_device(): summed = lax.psum(proj, 'blk')]
  transfers between devices with their start and end apart: 2 -> 16, of which waited for: 2 -> 8; matrix products, arithmetic and copies ran while one was open for 22% -> 21% of each run, Pallas kernels for 0% -> 0%
where the time goes in v1:
time: 423 us
  waiting for transfers between devices  144 us (34%)
  starting transfers between devices  110 us (26%)
  matrix products  90.9 us (21%)
  local copies, waits for them, and re-layouts  61.9 us (15%)
  between operations  14.2 us (3%)
    ppermute x8, starting transfers between devices, collect(): lower.append(lax.ppermute(lower[-1] if lower else x, axis, pairs))  105 us
    psum x1, waiting for transfers between devices, per_device(): summed = lax.psum(proj, 'blk')  93 us
    dot_general x1, matrix products, per_device(): jnp.einsum('rkast,rsu->rkatu', dipole, upper_blocks, preferred_element_ty...  58.2 us
    ppermute x8, waiting for transfers between devices, collect(): lower.append(lax.ppermute(lower[-1] if lower else x, axis, pairs))  50.8 us
    unnamed x55, local copies, waits for them, and re-layouts  33.5 us
    dot_general x1, matrix products, per_device(): jnp.einsum('eatu,etl->aul', halves, lows, preferred_element_type=jnp.floa...  32.7 us
    gather x1, local copies, waits for them, and re-layouts, per_device(): lows = jnp.take(all_blocks, columns, axis=0)  14 us
    gather x1, local copies, waits for them, and re-layouts, collect(): blocks = blocks[(jnp.arange(size) - shift) % size]  13.1 us
  transfers between devices with their start and end apart: 16, of which 8 were waited for; matrix products, arithmetic and copies ran while one was open for 21% of the time, Pallas kernels for 0%

profile of v1, /device:TPU:0, one launch (start us, length us, event | category | flops | bytes accessed | tf_op | source)
XLA Modules:
  0.0 422.6 jit_solution(9914563709074976912)
XLA Ops:
  7.2 0.0 copy-start
  7.2 0.0 all-reduce.2.cloned.1.call-start
  7.2 0.5 collective-permute-start
  7.7 17.7 %collective-permute-done = bf16[4096,128]{1,0:T(8,128)(2,1)S(1)} collective-permute-done((bf16[4096,128]{1,0:T(8,128)(2,1)}, bf16[4096,128]{1,0:T(8,128)(2,1)S(1)}, u32[]{:S(2)}, u32[]{:S(2)}) %collective-permute-start) | collective-permute-done | bytes 1048608 | tf_op jit(solution)/shard_map/ppermute | solution.py:22
  25.4 1.0 copy-done.2
  26.4 0.0 collective-permute-start.1
  26.4 4.4 %collective-permute-start.8 = (bf16[4096,128]{1,0:T(8,128)(2,1)}, bf16[4096,128]{1,0:T(8,128)(2,1)S(1)}, u32[]{:S(2)}, u32[]{:S(2)}) collective-permute-start(bf16[4096,128]{1,0:T(8,128)(2,1)} %param.9), channel_id=1, source_target_pairs={{1,0},{2,1},{3,2},{4,3},{5,4},{6,5},{7,6},{8,7},{9,8},{10,9},{11,1... | collective-permute-start | bytes 3145736 | tf_op jit(solution)/shard_map/ppermute | solution.py:24
  30.9 12.6 %collective-permute-done.1 = bf16[4096,128]{1,0:T(8,128)(2,1)S(1)} collective-permute-done((bf16[4096,128]{1,0:T(8,128)(2,1)S(1)}, bf16[4096,128]{1,0:T(8,128)(2,1)S(1)}, u32[]{:S(2)}, u32[]{:S(2)}) %collective-permute-start.1) | collective-permute-done | bytes 1048608 | tf_op jit(solution)/shard_map/ppermute | solution.py:22
  43.4 5.3 %collective-permute-start.2 = (bf16[4096,128]{1,0:T(8,128)(2,1)S(1)}, bf16[4096,128]{1,0:T(8,128)(2,1)S(1)}, u32[]{:S(2)}, u32[]{:S(2)}) collective-permute-start(bf16[4096,128]{1,0:T(8,128)(2,1)S(1)} %collective-permute-done.1), channel_id=1, source_target_pairs={{0,1},{1,2},{2,3},{3,4},{4,5},{5,6},{6,7},{7,8},{8,9},{9,10},{10,1... | collective-permute-start | bytes 3145736 | tf_op jit(solution)/shard_map/ppermute | solution.py:22
  48.8 0.0 collective-permute-done.8
  48.8 1.0 copy-done.3
  49.8 0.0 collective-permute-start.9
  49.8 10.7 %collective-permute-done.2 = bf16[4096,128]{1,0:T(8,128)(2,1)S(1)} collective-permute-done((bf16[4096,128]{1,0:T(8,128)(2,1)S(1)}, bf16[4096,128]{1,0:T(8,128)(2,1)S(1)}, u32[]{:S(2)}, u32[]{:S(2)}) %collective-permute-start.2) | collective-permute-done | bytes 1048608 | tf_op jit(solution)/shard_map/ppermute | solution.py:22
  60.5 13.8 %collective-permute-start.3 = (bf16[4096,128]{1,0:T(8,128)(2,1)S(1)}, bf16[4096,128]{1,0:T(8,128)(2,1)S(1)}, u32[]{:S(2)}, u32[]{:S(2)}) collective-permute-start(bf16[4096,128]{1,0:T(8,128)(2,1)S(1)} %collective-permute-done.2), channel_id=1, source_target_pairs={{0,1},{1,2},{2,3},{3,4},{4,5},{5,6},{6,7},{7,8},{8,9},{9,10},{10,1... | collective-permute-start | bytes 3145736 | tf_op jit(solution)/shard_map/ppermute | solution.py:22
  74.2 0.0 collective-permute-done.9
  74.2 0.1 collective-permute-start.10
  74.3 1.0 copy-done.6
  75.3 3.8 collective-permute-done.3
  79.1 19.9 %collective-permute-start.4 = (bf16[4096,128]{1,0:T(8,128)(2,1)S(1)}, bf16[4096,128]{1,0:T(8,128)(2,1)S(1)}, u32[]{:S(2)}, u32[]{:S(2)}) collective-permute-start(bf16[4096,128]{1,0:T(8,128)(2,1)S(1)} %collective-permute-done.3), channel_id=1, source_target_pairs={{0,1},{1,2},{2,3},{3,4},{4,5},{5,6},{6,7},{7,8},{8,9},{9,10},{10,1... | collective-permute-start | bytes 3145736 | tf_op jit(solution)/shard_map/ppermute | solution.py:22
  99.0 0.0 collective-permute-done.10
  99.0 0.1 collective-permute-start.11
  99.0 0.9 copy-done.9
  100.0 2.4 collective-permute-done.4
  102.4 21.4 %collective-permute-start.5 = (bf16[4096,128]{1,0:T(8,128)(2,1)S(1)}, bf16[4096,128]{1,0:T(8,128)(2,1)S(1)}, u32[]{:S(2)}, u32[]{:S(2)}) collective-permute-start(bf16[4096,128]{1,0:T(8,128)(2,1)S(1)} %collective-permute-done.4), channel_id=1, source_target_pairs={{0,1},{1,2},{2,3},{3,4},{4,5},{5,6},{6,7},{7,8},{8,9},{9,10},{10,1... | collective-permute-start | bytes 3145736 | tf_op jit(solution)/shard_map/ppermute | solution.py:22
  123.7 0.0 collective-permute-done.11
  123.7 1.0 copy-done.11
  124.7 0.0 collective-permute-start.12
  124.7 1.3 collective-permute-done.5
  126.0 22.3 %collective-permute-start.6 = (bf16[4096,128]{1,0:T(8,128)(2,1)S(1)}, bf16[4096,128]{1,0:T(8,128)(2,1)}, u32[]{:S(2)}, u32[]{:S(2)}) collective-permute-start(bf16[4096,128]{1,0:T(8,128)(2,1)S(1)} %collective-permute-done.5), channel_id=1, source_target_pairs={{0,1},{1,2},{2,3},{3,4},{4,5},{5,6},{6,7},{7,8},{8,9},{9,10},{10,1... | collective-permute-start | bytes 3145736 | tf_op jit(solution)/shard_map/ppermute | solution.py:22
  148.3 0.0 collective-permute-done.12
  148.3 0.0 collective-permute-start.13
  148.3 2.4 collective-permute-done.6
  150.7 22.2 %collective-permute-start.7 = (bf16[4096,128]{1,0:T(8,128)(2,1)}, bf16[4096,128]{1,0:T(8,128)(2,1)}, u32[]{:S(2)}, u32[]{:S(2)}) collective-permute-start(bf16[4096,128]{1,0:T(8,128)(2,1)} %collective-permute-done.6), channel_id=1, source_target_pairs={{0,1},{1,2},{2,3},{3,4},{4,5},{5,6},{6,7},{7,8},{8,9},{9,10},{10,1... | collective-permute-start | bytes 3145736 | tf_op jit(solution)/shard_map/ppermute | solution.py:22
  173.0 58.2 %convolution_convert_fusion = bf16[16,12,3,256,256]{4,3,2,1,0:T(8,128)(2,1)} fusion(bf16[16,12,3,256,256]{4,3,2,1,0:T(8,128)(2,1)} %param.6, bf16[16,256,256,1,1]{2,1,4,3,0:T(8,128)(2,1)S(1)} %bitcast.54), kind=kOutput, calls=%fused_computation.2 | convolution fusion | flops 19365101568 | bytes 153092096 | tf_op jit(solution)/shard_map/rkast,rsu->rkatu/dot_general | solution.py:36
  231.2 0.1 reshape.104
  231.3 0.1 reshape.103
  231.5 0.1 dynamic_slice.7
  231.6 0.0 collective-permute-done.13
  231.6 0.2 collective-permute-start.14
  231.9 0.0 collective-permute-done.7
  231.9 2.6 bitcast_dynamic-update-slice_fusion.15
  234.5 2.3 bitcast_dynamic-update-slice_fusion.14
  236.8 2.3 bitcast_dynamic-update-slice_fusion.13
  239.1 2.3 bitcast_dynamic-update-slice_fusion.12
  241.3 2.3 bitcast_dynamic-update-slice_fusion.11
  243.7 2.3 bitcast_dynamic-update-slice_fusion.10
  246.0 2.3 bitcast_dynamic-update-slice_fusion.9
  248.2 2.3 bitcast_dynamic-update-slice_fusion.8
  250.5 1.1 bitcast_dynamic-update-slice_fusion.7
  251.6 1.1 bitcast_dynamic-update-slice_fusion.6
  252.7 1.0 bitcast_dynamic-update-slice_fusion.5
  253.7 1.1 bitcast_dynamic-update-slice_fusion.4
  254.8 1.0 bitcast_dynamic-update-slice_fusion.3
  255.8 2.3 bitcast_dynamic-update-slice_fusion.2
  258.1 2.3 bitcast_dynamic-update-slice_fusion.1
  260.4 0.0 collective-permute-done.14
  260.4 1.1 bitcast_dynamic-update-slice_fusion
  261.5 13.1 %gather_fusion = bf16[16,4096,128]{2,1,0:T(8,128)(2,1)} fusion(bf16[16,4096,128]{2,1,0:T(8,128)(2,1)} %bitcast_dynamic-update-slice_fusion, s32[1024]{0:T(1024)S(1)} %pad_clamp_fusion.1), kind=kCustom, calls=%fused_computation | custom fusion | bytes 33554496 | tf_op jit(solution)/shard_map/gather | solution.py:27
  274.6 14.0 %gather_fusion.1 = bf16[192,256,128]{2,1,0:T(8,128)(2,1)} fusion(bf16[256,256,128]{2,1,0:T(8,128)(2,1)} %bitcast.55, s32[1024]{0:T(1024)S(1)} %pad_clamp_fusion), kind=kCustom, calls=%fused_computation.1 | custom fusion | bytes 25166592 | tf_op jit(solution)/shard_map/jit(_take)/gather | solution.py:46
  288.6 32.7 %fusion.5 = f32[3,256,128]{2,1,0:T(8,128)} fusion(bf16[192,3,256,256]{3,2,1,0:T(8,128)(2,1)} %bitcast.3, bf16[192,256,128]{2,1,0:T(8,128)(2,1)} %gather_fusion.1, pred[192]{0:T(512)(128)(4,1)S(1)} %compare_and_fusion), kind=kOutput, calls=%fused_computation.8 | convolution fusion | flops 9669967872 | bytes 88473792 | tf_op jit(solution)/shard_map/eatu,etl->aul/dot_general | solution.py:47
  321.3 0.0 all-reduce.2.cloned.1.call-update
  321.3 93.0 %all-reduce.2.cloned.1.call-done = f32[3,256,128]{2,1,0:T(8,128)} async-done(((f32[3,256,128]{2,1,0:T(8,128)}), f32[3,256,128]{2,1,0:T(8,128)}) %all-reduce.2.cloned.1.call-update) | async-done | bytes 393232 | tf_op jit(solution)/shard_map/psum | solution.py:50
  414.3 0.7 multiply_reduce_fusion
  415.1 0.7 fusion.9
  (40 shorter events, 0.1 us)
Async XLA Ops:
  7.2 165.8 %copy-start = (bf16[4096,256]{1,0:T(8,128)(2,1)S(1)}, bf16[4096,256]{1,0:T(8,128)(2,1)}, u32[]{:S(2)}) copy-start(bf16[4096,256]{1,0:T(8,128)(2,1)} %param.8) | copy-start | bytes 6291460
  7.2 407.1 %all-reduce.2.cloned.1.call-start = ((), (), s32[]{:S(2)}) async-start(), calls=%async_computation | async-start | bytes 786432 | tf_op jit(solution)/shard_map/psum | solution.py:50
  7.2 18.2 %collective-permute-start = (bf16[4096,128]{1,0:T(8,128)(2,1)}, bf16[4096,128]{1,0:T(8,128)(2,1)S(1)}, u32[]{:S(2)}, u32[]{:S(2)}) collective-permute-start(bf16[4096,128]{1,0:T(8,128)(2,1)} %param.9), channel_id=1, source_target_pairs={{0,1},{1,2},{2,3},{3,4},{4,5},{5,6},{6,7},{7,8},{8,9},{9,10},{10,1... | collective-permute-start | bytes 3145736 | tf_op jit(solution)/shard_map/ppermute | solution.py:22
  25.4 1.0 copy-start.2
  26.4 17.0 %collective-permute-start.1 = (bf16[4096,128]{1,0:T(8,128)(2,1)S(1)}, bf16[4096,128]{1,0:T(8,128)(2,1)S(1)}, u32[]{:S(2)}, u32[]{:S(2)}) collective-permute-start(bf16[4096,128]{1,0:T(8,128)(2,1)S(1)} %collective-permute-done), channel_id=1, source_target_pairs={{0,1},{1,2},{2,3},{3,4},{4,5},{5,6},{6,7},{7,8},{8,9},{9,10},{10,1... | collective-permute-start | bytes 3145736 | tf_op jit(solution)/shard_map/ppermute | solution.py:22
  26.4 22.4 %collective-permute-start.8 = (bf16[4096,128]{1,0:T(8,128)(2,1)}, bf16[4096,128]{1,0:T(8,128)(2,1)S(1)}, u32[]{:S(2)}, u32[]{:S(2)}) collective-permute-start(bf16[4096,128]{1,0:T(8,128)(2,1)} %param.9), channel_id=1, source_target_pairs={{1,0},{2,1},{3,2},{4,3},{5,4},{6,5},{7,6},{8,7},{9,8},{10,9},{11,1... | collective-permute-start | bytes 3145736 | tf_op jit(solution)/shard_map/ppermute | solution.py:24
  43.4 30.8 %copy-start.5 = (bf16[4096,128]{1,0:T(8,128)(2,1)}, bf16[4096,128]{1,0:T(8,128)(2,1)S(1)}, u32[]{:S(2)}) copy-start(bf16[4096,128]{1,0:T(8,128)(2,1)S(1)} %collective-permute-done.1) | copy-start | bytes 3145732
  43.4 17.0 %collective-permute-start.2 = (bf16[4096,128]{1,0:T(8,128)(2,1)S(1)}, bf16[4096,128]{1,0:T(8,128)(2,1)S(1)}, u32[]{:S(2)}, u32[]{:S(2)}) collective-permute-start(bf16[4096,128]{1,0:T(8,128)(2,1)S(1)} %collective-permute-done.1), channel_id=1, source_target_pairs={{0,1},{1,2},{2,3},{3,4},{4,5},{5,6},{6,7},{7,8},{8,9},{9,10},{10,1... | collective-permute-start | bytes 3145736 | tf_op jit(solution)/shard_map/ppermute | solution.py:22
  48.8 1.0 copy-start.3
  49.8 24.5 %collective-permute-start.9 = (bf16[4096,128]{1,0:T(8,128)(2,1)S(1)}, bf16[4096,128]{1,0:T(8,128)(2,1)S(1)}, u32[]{:S(2)}, u32[]{:S(2)}) collective-permute-start(bf16[4096,128]{1,0:T(8,128)(2,1)S(1)} %collective-permute-done.8), channel_id=1, source_target_pairs={{1,0},{2,1},{3,2},{4,3},{5,4},{6,5},{7,6},{8,7},{9,8},{10,9},{11,1... | collective-permute-start | bytes 3145736 | tf_op jit(solution)/shard_map/ppermute | solution.py:24
  60.5 38.5 %copy-start.8 = (bf16[4096,128]{1,0:T(8,128)(2,1)}, bf16[4096,128]{1,0:T(8,128)(2,1)S(1)}, u32[]{:S(2)}) copy-start(bf16[4096,128]{1,0:T(8,128)(2,1)S(1)} %collective-permute-done.2) | copy-start | bytes 3145732
  60.5 18.6 %collective-permute-start.3 = (bf16[4096,128]{1,0:T(8,128)(2,1)S(1)}, bf16[4096,128]{1,0:T(8,128)(2,1)S(1)}, u32[]{:S(2)}, u32[]{:S(2)}) collective-permute-start(bf16[4096,128]{1,0:T(8,128)(2,1)S(1)} %collective-permute-done.2), channel_id=1, source_target_pairs={{0,1},{1,2},{2,3},{3,4},{4,5},{5,6},{6,7},{7,8},{8,9},{9,10},{10,1... | collective-permute-start | bytes 3145736 | tf_op jit(solution)/shard_map/ppermute | solution.py:22
  74.2 1.0 copy-start.6
  74.2 24.7 %collective-permute-start.10 = (bf16[4096,128]{1,0:T(8,128)(2,1)S(1)}, bf16[4096,128]{1,0:T(8,128)(2,1)S(1)}, u32[]{:S(2)}, u32[]{:S(2)}) collective-permute-start(bf16[4096,128]{1,0:T(8,128)(2,1)S(1)} %collective-permute-done.9), channel_id=1, source_target_pairs={{1,0},{2,1},{3,2},{4,3},{5,4},{6,5},{7,6},{8,7},{9,8},{10,9},{11,1... | collective-permute-start | bytes 3145736 | tf_op jit(solution)/shard_map/ppermute | solution.py:24
  79.0 69.3 %copy-start.13 = (bf16[4096,128]{1,0:T(8,128)(2,1)}, bf16[4096,128]{1,0:T(8,128)(2,1)S(1)}, u32[]{:S(2)}) copy-start(bf16[4096,128]{1,0:T(8,128)(2,1)S(1)} %collective-permute-done.3) | copy-start | bytes 3145732
  79.1 23.3 %collective-permute-start.4 = (bf16[4096,128]{1,0:T(8,128)(2,1)S(1)}, bf16[4096,128]{1,0:T(8,128)(2,1)S(1)}, u32[]{:S(2)}, u32[]{:S(2)}) collective-permute-start(bf16[4096,128]{1,0:T(8,128)(2,1)S(1)} %collective-permute-done.3), channel_id=1, source_target_pairs={{0,1},{1,2},{2,3},{3,4},{4,5},{5,6},{6,7},{7,8},{8,9},{9,10},{10,1... | collective-permute-start | bytes 3145736 | tf_op jit(solution)/shard_map/ppermute | solution.py:22
  99.0 1.0 copy-start.9
  99.0 24.7 %collective-permute-start.11 = (bf16[4096,128]{1,0:T(8,128)(2,1)S(1)}, bf16[4096,128]{1,0:T(8,128)(2,1)S(1)}, u32[]{:S(2)}, u32[]{:S(2)}) collective-permute-start(bf16[4096,128]{1,0:T(8,128)(2,1)S(1)} %collective-permute-done.10), channel_id=1, source_target_pairs={{1,0},{2,1},{3,2},{4,3},{5,4},{6,5},{7,6},{8,7},{9,8},{10,9},{11,1... | collective-permute-start | bytes 3145736 | tf_op jit(solution)/shard_map/ppermute | solution.py:24
  102.4 45.9 %copy-start.14 = (bf16[4096,128]{1,0:T(8,128)(2,1)}, bf16[4096,128]{1,0:T(8,128)(2,1)S(1)}, u32[]{:S(2)}) copy-start(bf16[4096,128]{1,0:T(8,128)(2,1)S(1)} %collective-permute-done.4) | copy-start | bytes 3145732
  102.4 23.6 %collective-permute-start.5 = (bf16[4096,128]{1,0:T(8,128)(2,1)S(1)}, bf16[4096,128]{1,0:T(8,128)(2,1)S(1)}, u32[]{:S(2)}, u32[]{:S(2)}) collective-permute-start(bf16[4096,128]{1,0:T(8,128)(2,1)S(1)} %collective-permute-done.4), channel_id=1, source_target_pairs={{0,1},{1,2},{2,3},{3,4},{4,5},{5,6},{6,7},{7,8},{8,9},{9,10},{10,1... | collective-permute-start | bytes 3145736 | tf_op jit(solution)/shard_map/ppermute | solution.py:22
  123.7 1.0 copy-start.11
  124.7 23.6 %collective-permute-start.12 = (bf16[4096,128]{1,0:T(8,128)(2,1)S(1)}, bf16[4096,128]{1,0:T(8,128)(2,1)}, u32[]{:S(2)}, u32[]{:S(2)}) collective-permute-start(bf16[4096,128]{1,0:T(8,128)(2,1)S(1)} %collective-permute-done.11), channel_id=1, source_target_pairs={{1,0},{2,1},{3,2},{4,3},{5,4},{6,5},{7,6},{8,7},{9,8},{10,9},{11,1... | collective-permute-start | bytes 3145736 | tf_op jit(solution)/shard_map/ppermute | solution.py:24
  126.0 24.7 %copy-start.15 = (bf16[4096,128]{1,0:T(8,128)(2,1)}, bf16[4096,128]{1,0:T(8,128)(2,1)S(1)}, u32[]{:S(2)}) copy-start(bf16[4096,128]{1,0:T(8,128)(2,1)S(1)} %collective-permute-done.5) | copy-start | bytes 3145732
  126.0 24.7 %collective-permute-start.6 = (bf16[4096,128]{1,0:T(8,128)(2,1)S(1)}, bf16[4096,128]{1,0:T(8,128)(2,1)}, u32[]{:S(2)}, u32[]{:S(2)}) collective-permute-start(bf16[4096,128]{1,0:T(8,128)(2,1)S(1)} %collective-permute-done.5), channel_id=1, source_target_pairs={{0,1},{1,2},{2,3},{3,4},{4,5},{5,6},{6,7},{7,8},{8,9},{9,10},{10,1... | collective-permute-start | bytes 3145736 | tf_op jit(solution)/shard_map/ppermute | solution.py:22
  148.3 83.3 %collective-permute-start.13 = (bf16[4096,128]{1,0:T(8,128)(2,1)}, bf16[4096,128]{1,0:T(8,128)(2,1)}, u32[]{:S(2)}, u32[]{:S(2)}) collective-permute-start(bf16[4096,128]{1,0:T(8,128)(2,1)} %collective-permute-done.12), channel_id=1, source_target_pairs={{1,0},{2,1},{3,2},{4,3},{5,4},{6,5},{7,6},{8,7},{9,8},{10,9},{11,1... | collective-permute-start | bytes 3145736 | tf_op jit(solution)/shard_map/ppermute | solution.py:24
  150.7 81.1 %collective-permute-start.7 = (bf16[4096,128]{1,0:T(8,128)(2,1)}, bf16[4096,128]{1,0:T(8,128)(2,1)}, u32[]{:S(2)}, u32[]{:S(2)}) collective-permute-start(bf16[4096,128]{1,0:T(8,128)(2,1)} %collective-permute-done.6), channel_id=1, source_target_pairs={{0,1},{1,2},{2,3},{3,4},{4,5},{5,6},{6,7},{7,8},{8,9},{9,10},{10,1... | collective-permute-start | bytes 3145736 | tf_op jit(solution)/shard_map/ppermute | solution.py:22
  173.0 58.2 %copy-start.16 = (s32[16,12]{1,0:T(8,128)S(1)}, s32[16,12]{1,0:T(8,128)}, u32[]{:S(2)}) copy-start(s32[16,12]{1,0:T(8,128)} %param.7) | copy-start | bytes 2308
  173.0 58.4 %copy-start.19 = (f32[256]{0:T(256)S(1)}, f32[256]{0:T(256)}, u32[]{:S(2)}) copy-start(f32[256]{0:T(256)} %param.10) | copy-start | bytes 3076
  231.2 19.3 %copy-start.1 = (bf16[4096,128]{1,0:T(8,128)(2,1)S(1)}, bf16[4096,128]{1,0:T(8,128)(2,1)}, u32[]{:S(2)}) copy-start(bf16[4096,128]{1,0:T(8,128)(2,1)} %param.9) | copy-start | bytes 3145732
  231.4 20.2 %copy-start.4 = (bf16[4096,128]{1,0:T(8,128)(2,1)S(1)}, bf16[4096,128]{1,0:T(8,128)(2,1)}, u32[]{:S(2)}) copy-start(bf16[4096,128]{1,0:T(8,128)(2,1)} %copy-done.3) | copy-start | bytes 3145732
  231.4 21.3 %copy-start.7 = (bf16[4096,128]{1,0:T(8,128)(2,1)S(1)}, bf16[4096,128]{1,0:T(8,128)(2,1)}, u32[]{:S(2)}) copy-start(bf16[4096,128]{1,0:T(8,128)(2,1)} %copy-done.6) | copy-start | bytes 3145732
  231.4 22.3 %copy-start.10 = (bf16[4096,128]{1,0:T(8,128)(2,1)S(1)}, bf16[4096,128]{1,0:T(8,128)(2,1)}, u32[]{:S(2)}) copy-start(bf16[4096,128]{1,0:T(8,128)(2,1)} %copy-done.9) | copy-start | bytes 3145732
  231.4 23.3 %copy-start.12 = (bf16[4096,128]{1,0:T(8,128)(2,1)S(1)}, bf16[4096,128]{1,0:T(8,128)(2,1)}, u32[]{:S(2)}) copy-start(bf16[4096,128]{1,0:T(8,128)(2,1)} %copy-done.11) | copy-start | bytes 3145732
  231.6 28.8 %collective-permute-start.14 = (bf16[4096,128]{1,0:T(8,128)(2,1)}, bf16[4096,128]{1,0:T(8,128)(2,1)S(1)}, u32[]{:S(2)}, u32[]{:S(2)}) collective-permute-start(bf16[4096,128]{1,0:T(8,128)(2,1)} %collective-permute-done.13), channel_id=1, source_target_pairs={{1,0},{2,1},{3,2},{4,3},{5,4},{6,5},{7,6},{8,7},{9,8},{10,9},{11,1... | collective-permute-start | bytes 3145736 | tf_op jit(solution)/shard_map/ppermute | solution.py:24
  288.6 32.7 %copy-start.18 = (f32[128]{0:T(128)S(1)}, f32[128]{0:T(128)}, u32[]{:S(2)}) copy-start(f32[128]{0:T(128)} %param.11) | copy-start | bytes 1540
  415.1 0.7 copy-start.17
Sparse Core Ops, SparseCore 0:
  321.4 92.8 all-reduce.1
